TPU v7x, 512 devices: a whole 4x8x8 slice. The times are simulated.
512 devices in a mesh: segment: 32 (over y_lo, z), dp: 8 (over x, core), seq: 2 (over y_hi).
Axes of the slice: x: 4, y: 8 (y_hi: 2, y_lo: 4; y = y_hi * 4 + y_lo), z: 8, core: 2. Of those that a mesh axis runs over, the one named last changes fastest.
Arguments:
- stored_part_activation: bfloat16 [32, 2, 8, 256, 2048], P('segment', None, 'dp', 'seq'), may hold values from -64 to 64
- pending_sensitivity: bfloat16 [32, 8, 256, 2048], P('segment', 'dp', 'seq'), may hold values from -0.119628906 to 0.119628906
- uppermost_result_derivative: bfloat16 [1, 8, 256, 2048], P(None, 'dp', 'seq'), may hold values from -0.119628906 to 0.119628906
- scaling_factors: float32 [32, 4, 2048], P('segment'), may hold values from -0.5 to 5
- attended_tile_table: int32 [32, 2, 8, 2, 2], P('segment', None, 'dp'), may hold values from 0 to 1, as said below
- active_tile_number: int32 [32, 2, 8, 2], P('segment', None, 'dp'), may hold values from 1 to 2
Outputs:
- factor_derivatives: float32 [32, 4, 2048], P('segment')
Inputs may be any that keep to these rules, and one draw needn't show every extreme that they name: `attended_tile_table`: each list names every key block of its sample once; the allowed ones come first.
All inputs are finite; a program needn't handle non-finite values.
Results may differ from a plain program's by a relative error of at most 0.009.
Values may be sent and summed in bfloat16 or wider, within the bound.
A program may use at most 64 MiB of HBM per device.

v0:
```python
import jax
import jax.numpy as jnp
from jax import lax
from jax.sharding import PartitionSpec as P

HEAD_DIM = 128
BLK = 128
epsilon = 1e-06


def partner(block, axis, apart):
    count = lax.axis_size(axis)
    route = []
    for low in range(count):
        high = low | 1 << apart
        if high != low and high < count:
            route += [(low, high), (high, low)]
    return lax.ppermute(block, axis, route)


def from_behind(block, axis, distance):
    devices = range(lax.axis_size(axis))
    route = [(i - distance, i) for i in devices if i - distance in devices]
    return lax.ppermute(block, axis, route)


def normed_of(inputs):
    widened = inputs.astype(jnp.float32).reshape(
        inputs.shape[:-1] + (inputs.shape[-1] // HEAD_DIM, HEAD_DIM)
    )
    inv_rms = lax.rsqrt(jnp.mean(widened * widened, axis=-1, keepdims=True) + epsilon)
    return (widened * inv_rms, inv_rms)


def norm_back(grad_norm, norm_val, inv_rms):
    return inv_rms * (grad_norm - norm_val * jnp.mean(grad_norm * norm_val, axis=-1, keepdims=True))


def allowed_blocks(block_list, live_count):
    block_total = block_list.shape[0]
    live_slots = jnp.arange(block_total)[None, :] < live_count[:, None]
    matches = (block_list[:, :, None] == jnp.arange(block_total)[None, None, :]) & live_slots[
        :, :, None
    ]
    return jnp.any(matches, axis=1)


def token_mask(permitted, query_half, seq_index, dev_blocks):
    local_blocks = jnp.arange(dev_blocks, dtype=jnp.int32)
    query_rows = query_half * dev_blocks + local_blocks
    key_order = jnp.concatenate(
        [seq_index * dev_blocks + local_blocks, (1 - seq_index) * dev_blocks + local_blocks]
    )
    picked = permitted[query_rows[:, None], key_order[None, :]]
    return jnp.repeat(jnp.repeat(picked, BLK, axis=0), BLK, axis=1)


def attend(query_norm, key_norm, gain_heads, allowed, incoming, scaling):
    queries = (query_norm * gain_heads[0]).astype(jnp.bfloat16)
    key_mat = (key_norm * gain_heads[1]).astype(jnp.bfloat16)
    val_mat = (key_norm * gain_heads[2]).astype(jnp.bfloat16)
    scores = (
        jnp.einsum("thd,shd->hts", queries, key_mat, preferred_element_type=jnp.float32) * scaling
    )
    scores = jnp.where(allowed[None], scores, -jnp.inf)
    exped = jnp.exp(scores - jnp.max(scores, axis=-1, keepdims=True))
    probs = exped / jnp.sum(exped, axis=-1, keepdims=True)
    probs_low = probs.astype(jnp.bfloat16)
    output = jnp.einsum("hts,shd->thd", probs_low, val_mat, preferred_element_type=jnp.float32)
    grad_out = (gain_heads[3] * incoming).astype(jnp.bfloat16)
    grad_probs = jnp.einsum("thd,shd->hts", grad_out, val_mat, preferred_element_type=jnp.float32)
    grad_scores = (
        probs * (grad_probs - jnp.sum(probs * grad_probs, axis=-1, keepdims=True))
    ).astype(jnp.bfloat16)
    return (queries, key_mat, probs_low, output, grad_out, grad_scores)


def shards(
    stored_part_activation,
    pending_sensitivity,
    uppermost_result_derivative,
    scaling_factors,
    attended_tile_table,
    active_tile_number,
):
    segments = lax.axis_size("segment")
    segment_index = lax.axis_index("segment")
    seq_index = lax.axis_index("seq")
    window = stored_part_activation.shape[1]
    row_count = stored_part_activation.shape[3]
    channels = stored_part_activation.shape[4]
    head_count = channels // HEAD_DIM
    dev_blocks = row_count // BLK
    scaling = HEAD_DIM ** (-0.5)
    own_window = stored_part_activation[0, :, 0]
    gain_heads = scaling_factors[0].reshape(4, head_count, HEAD_DIM)
    incoming_sensitivity = pending_sensitivity[0, 0].astype(jnp.float32)
    totals = jnp.zeros((4, head_count, HEAD_DIM), jnp.float32)
    for step_index in range(window):
        own_rows = own_window[step_index]
        other_rows = partner(own_rows, "seq", 0)
        permitted = allowed_blocks(
            attended_tile_table[0, step_index, 0], active_tile_number[0, step_index, 0]
        )
        own_norm, own_inv = normed_of(own_rows)
        other_norm, other_inv = normed_of(other_rows)
        key_norm = jnp.concatenate([own_norm, other_norm], axis=0)
        incoming = incoming_sensitivity.reshape(row_count, head_count, HEAD_DIM)
        own_allowed = token_mask(permitted, seq_index, seq_index, dev_blocks)
        queries, key_mat, probs_low, output, grad_out, grad_scores = attend(
            own_norm, key_norm, gain_heads, own_allowed, incoming, scaling
        )
        grad_query = (
            jnp.einsum("hts,shd->thd", grad_scores, key_mat, preferred_element_type=jnp.float32)
            * scaling
        )
        grad_key = (
            jnp.einsum("hts,thd->shd", grad_scores, queries, preferred_element_type=jnp.float32)
            * scaling
        )
        grad_value = jnp.einsum(
            "hts,thd->shd", probs_low, grad_out, preferred_element_type=jnp.float32
        )
        key_part = grad_key * gain_heads[1] + grad_value * gain_heads[2]
        self_part = key_part[:row_count]
        key_terms = jnp.sum(grad_key * key_norm, axis=0)
        value_terms = jnp.sum(grad_value * key_norm, axis=0)
        if step_index < window - 1:
            lent = norm_back(key_part[row_count:], other_norm, other_inv).astype(jnp.bfloat16)
            returned = partner(lent, "seq", 0).astype(jnp.float32)
        grad_terms = jnp.stack(
            [
                jnp.sum(grad_query * own_norm, axis=0),
                key_terms,
                value_terms,
                jnp.sum(output * incoming, axis=0),
            ]
        )
        totals = totals + grad_terms
        if step_index < window - 1:
            grad_input = (
                incoming
                + norm_back(grad_query * gain_heads[0] + self_part, own_norm, own_inv)
                + returned
            )
            received = from_behind(grad_input.reshape(row_count, channels), "segment", -1)
            incoming_sensitivity = jnp.where(
                segment_index == segments - 1,
                uppermost_result_derivative[step_index, 0].astype(jnp.float32),
                received,
            )
    summed = lax.psum(totals.reshape(4, channels), ("dp", "seq"))
    return summed[None]


def solution(mesh):
    placed = (
        P("segment", None, "dp", "seq", None),
        P("segment", "dp", "seq", None),
        P(None, "dp", "seq", None),
        P("segment", None, None),
        P("segment", None, "dp", None, None),
        P("segment", None, "dp", None),
    )
    return jax.shard_map(
        shards, mesh=mesh, in_specs=placed, out_specs=P("segment", None, None), check_vma=False
    )
```

profile of v0, /device:TPU:24, one launch (start us, length us, event | category | flops | bytes accessed | tf_op | source)
XLA Modules:
  0.0 220.2 jit_solution(2187491883206557950)
XLA Ops:
  0.0 2.7 %slice_convert_fusion = (f32[1,1,1,128,2048]{4,3,2,1,0:T(8,128)}, bf16[128,2048]{1,0:T(8,128)(2,1)}, bf16[128,2048]{1,0:T(8,128)(2,1)}, f32[1,1,1,128,2048]{4,3,2,1,0:T(8,128)S(1)}) fusion(bf16[1,2,1,128,2048]{4,3,2,1,0:T(8,128)(2,1)} %param.6), kind=kLoop, calls=%fused_computation.75 | loop fusion | flops 524288 | bytes 4194304 | tf_op jit(solution)/shard_map/convert_element_type | solution.py:28
  2.7 5.0 %collective-permute-start = (bf16[128,2048]{1,0:T(8,128)(2,1)}, bf16[128,2048]{1,0:T(8,128)(2,1)}, u32[]{:S(2)}, u32[]{:S(2)}) collective-permute-start(bf16[128,2048]{1,0:T(8,128)(2,1)} %get-tuple-element.12), channel_id=1, source_target_pairs={{0,1},{1,0},{2,3},{3,2},{4,5},{5,4},{6,7},{7,6},{8,9},{9,8},{10,11... | collective-permute-start | bytes 1572872 | tf_op jit(solution)/shard_map/ppermute | solution.py:18
  7.8 4.7 %collective-permute-start.1 = (bf16[128,2048]{1,0:T(8,128)(2,1)}, bf16[128,2048]{1,0:T(8,128)(2,1)}, u32[]{:S(2)}, u32[]{:S(2)}) collective-permute-start(bf16[128,2048]{1,0:T(8,128)(2,1)} %get-tuple-element.13), channel_id=1, source_target_pairs={{0,1},{1,0},{2,3},{3,2},{4,5},{5,4},{6,7},{7,6},{8,9},{9,8},{10,11... | collective-permute-start | bytes 1572872 | tf_op jit(solution)/shard_map/ppermute | solution.py:18
  14.8 1.5 copy.58
  16.6 2.3 %copy.53 = f32[1,1,128,2048]{2,3,1,0:T(8,128)} copy(bf16[1,1,128,2048]{3,2,1,0:T(8,128)(2,1)} %param.7) | data formatting | bytes 1572864 | tf_op jit(solution)/shard_map/convert_element_type | solution.py:97
  20.6 12.6 %collective-permute-done = bf16[128,2048]{1,0:T(8,128)(2,1)} collective-permute-done((bf16[128,2048]{1,0:T(8,128)(2,1)}, bf16[128,2048]{1,0:T(8,128)(2,1)}, u32[]{:S(2)}, u32[]{:S(2)}) %collective-permute-start) | collective-permute-done | bytes 524320 | tf_op jit(solution)/shard_map/ppermute | solution.py:18
  35.6 3.9 %fusion.49 = (f32[16,128]{1,0:T(8,128)S(1)}, f32[16,128,256]{2,1,0:T(8,128)}) fusion(pred[256]{0:T(512)(128)(4,1)S(1)} %broadcast_bitcast_fusion.1, f32[16,128]{1,0:T(8,128)S(1)} %bitcast.124, f32[128,16,128]{0,2,1:T(8,128)} %broadcast_multiply_fusion.2, f32[128,16,128]{0,2,1:T(8,128)S(1)} %broadcast_multiply_fusion.3, f32[16,128]{1,0:T(8,128)S(1)} %bitcast.119), kind=kOutput, calls=%fused_computation.119 | convolution fusion | flops 138412288 | bytes 4219136 | tf_op jit(solution)/shard_map/sub | solution.py:66
  39.5 2.8 %fusion.26 = f32[16,128,256]{2,1,0:T(8,128)S(1)} fusion(f32[128,16,128]{0,2,1:T(8,128)} %bitcast.110, f32[16,128]{1,0:T(8,128)S(1)} %bitcast.141, f32[16,128,256]{2,1,0:T(8,128)} %get-tuple-element.24, f32[16,128]{1,0:T(8,128)S(1)} %get-tuple-element.23), kind=kOutput, calls=%fused_computation.70 | convolution fusion | flops 135790592 | bytes 5259264 | tf_op jit(solution)/shard_map/hts,thd->shd/dot_general | solution.py:121
  42.7 2.2 multiply_reduce_fusion.1
  45.6 1.9 fusion.5
  47.6 1.9 multiply_reduce_fusion.3
  50.5 6.3 %collective-permute-start.2 = (bf16[128,16,128]{0,2,1:T(8,128)(2,1)}, bf16[128,16,128]{0,2,1:T(8,128)(2,1)}, u32[]{:S(2)}, u32[]{:S(2)}) collective-permute-start(bf16[128,16,128]{0,2,1:T(8,128)(2,1)} %multiply_convert_fusion.7), channel_id=1, source_target_pairs={{0,1},{1,0},{2,3},{3,2},{4,5},{5,4},{6,7},{7,6},{8,9},{9,8},{10,11... | collective-permute-start | bytes 1572872 | tf_op jit(solution)/shard_map/ppermute | solution.py:18
  56.9 1.2 copy.59
  58.2 22.9 %collective-permute-done.2 = bf16[128,16,128]{0,2,1:T(8,128)(2,1)} collective-permute-done((bf16[128,16,128]{0,2,1:T(8,128)(2,1)}, bf16[128,16,128]{0,2,1:T(8,128)(2,1)}, u32[]{:S(2)}, u32[]{:S(2)}) %collective-permute-start.2) | collective-permute-done | bytes 524320 | tf_op jit(solution)/shard_map/ppermute | solution.py:18
  81.1 3.6 %convert_add_fusion = f32[128,16,128]{0,2,1:T(8,128)} fusion(bf16[128,16,128]{0,2,1:T(8,128)(2,1)} %collective-permute-done.2, f32[128,16,128]{0,2,1:T(8,128)} %bitcast.111, f32[128,16]{0,1:T(8,128)S(1)} %broadcast_multiply_fusion.7, f32[128,16]{0,1:T(8,128)S(1)} %add_rsqrt_fusion.3, f32[256,16,128]{0,2,1:T(8,128)} %copy-done.2, ...), kind=kLoop, calls=%fused_computation.45 | loop fusion | flops 2359296 | bytes 5791744 | tf_op jit(solution)/shard_map/add | solution.py:142
  84.7 2.6 %copy.62 = f32[128,2048]{1,0:T(8,128)} copy(f32[128,2048]{0,1:T(8,128)} %bitcast.114) | data formatting | bytes 2097152 | tf_op jit(solution)/shard_map/reshape | solution.py:146
  87.3 11.7 %collective-permute-start.3 = (f32[128,2048]{1,0:T(8,128)}, f32[128,2048]{1,0:T(8,128)}, u32[]{:S(2)}, u32[]{:S(2)}) collective-permute-start(f32[128,2048]{1,0:T(8,128)} %copy.62), channel_id=1, source_target_pairs={{16,0},{32,16},{48,32},{64,48},{80,64},{96,80},{112,96},{128,112},... | collective-permute-start | bytes 3145736 | tf_op jit(solution)/shard_map/ppermute | solution.py:24
  100.1 4.8 %fusion.50 = (f32[16,128]{1,0:T(8,128)S(1)}, f32[16,128,256]{2,1,0:T(8,128)}) fusion(pred[256]{0:T(512)(128)(4,1)S(1)} %broadcast_bitcast_fusion, f32[16,128]{1,0:T(8,128)S(1)} %bitcast.126, f32[128,16,128]{0,2,1:T(8,128)} %broadcast_multiply_fusion, f32[128,16,128]{0,2,1:T(8,128)} %broadcast_multiply_fusion.1, f32[16,128]{1,0:T(8,128)S(1)} %bitcast.121), kind=kOutput, calls=%fused_computation.120 | convolution fusion | flops 138412288 | bytes 4219136 | tf_op jit(solution)/shard_map/sub | solution.py:66
  104.9 2.6 %fusion.12 = f32[16,128]{1,0:T(8,128)S(1)} fusion(f32[128,16,128]{0,2,1:T(8,128)S(1)} %bitcast.113, f32[16,128]{1,0:T(8,128)S(1)} %bitcast.133, f32[128,16,128]{0,2,1:T(8,128)S(1)} %copy-done.1, f32[128,16,128]{0,2,1:T(8,128)S(1)} %broadcast_multiply_fusion.3, f32[16,128,256]{2,1,0:T(8,128)} %get-tuple-element.24, f32[16,128]{1,0:T(8,128)S(1)} %get-tuple-element.23), kind=kOutput, calls=%fused_computation.37 | convolution fusion | flops 137361408 | bytes 5267456 | tf_op jit(solution)/shard_map/hts,shd->thd/dot_general | solution.py:69
  107.5 14.2 %collective-permute-done.3 = f32[128,2048]{1,0:T(8,128)} collective-permute-done((f32[128,2048]{1,0:T(8,128)}, f32[128,2048]{1,0:T(8,128)}, u32[]{:S(2)}, u32[]{:S(2)}) %collective-permute-start.3) | collective-permute-done | bytes 1048608 | tf_op jit(solution)/shard_map/ppermute | solution.py:24
  121.7 1.3 convert_select_fusion
  123.1 1.3 copy.63
  124.4 3.4 %multiply_reduce_fusion = (f32[16,128]{1,0:T(8,128)S(1)}, f32[16,128,256]{2,1,0:T(8,128)S(1)}) fusion(f32[16,128,256]{2,1,0:T(8,128)S(1)} %copy-done.6, f32[16,128]{1,0:T(8,128)S(1)} %get-tuple-element.28, f32[16,128]{1,0:T(8,128)S(1)} %bitcast.134, f32[128,16,128]{0,2,1:T(8,128)} %broadcast_multiply_fusion, f32[128,16,128]{0,2,1:T(8,128)} %broadcast_multiply_fusion.1, ...), kind=kOutput, calls=%fused_computation.17 | convolution fusion | flops 137885696 | bytes 7372800 | tf_op jit(solution)/shard_map/thd,shd->hts/dot_general | solution.py:71
  133.7 86.5 %psum.7 = f32[1,4,2048]{2,1,0:T(4,128)} all-reduce(f32[1,4,2048]{2,1,0:T(4,128)S(1)} %fusion.32), channel_id=1, replica_groups=mesh['segment'=32,'dp'=8,'seq'=2] {'dp','seq'}, use_global_device_ids=true, to_apply=%region_22.23 | all-reduce | flops 8192 | bytes 65536 | tf_op jit(solution)/shard_map/psum | solution.py:152
  (68 shorter events, 15.7 us)
Async XLA Ops:
  0.0 12.8 %copy-start.13 = (s32[1,2,1,2]{3,2,1,0:T(1,128)S(1)}, s32[1,2,1,2]{3,2,1,0:T(1,128)}, u32[]{:S(2)}) copy-start(s32[1,2,1,2]{3,2,1,0:T(1,128)} %param.11) | copy-start | bytes 52
  0.0 12.8 %copy-start.12 = (s32[1,2,1,2,2]{4,3,2,1,0:T(2,128)S(1)}, s32[1,2,1,2,2]{4,3,2,1,0:T(2,128)}, u32[]{:S(2)}) copy-start(s32[1,2,1,2,2]{4,3,2,1,0:T(2,128)} %param.10) | copy-start | bytes 100
  2.7 30.5 %collective-permute-start = (bf16[128,2048]{1,0:T(8,128)(2,1)}, bf16[128,2048]{1,0:T(8,128)(2,1)}, u32[]{:S(2)}, u32[]{:S(2)}) collective-permute-start(bf16[128,2048]{1,0:T(8,128)(2,1)} %get-tuple-element.12), channel_id=1, source_target_pairs={{0,1},{1,0},{2,3},{3,2},{4,5},{5,4},{6,7},{7,6},{8,9},{9,8},{10,11... | collective-permute-start | bytes 1572872 | tf_op jit(solution)/shard_map/ppermute | solution.py:18
  7.8 49.1 %collective-permute-start.1 = (bf16[128,2048]{1,0:T(8,128)(2,1)}, bf16[128,2048]{1,0:T(8,128)(2,1)}, u32[]{:S(2)}, u32[]{:S(2)}) collective-permute-start(bf16[128,2048]{1,0:T(8,128)(2,1)} %get-tuple-element.13), channel_id=1, source_target_pairs={{0,1},{1,0},{2,3},{3,2},{4,5},{5,4},{6,7},{7,6},{8,9},{9,8},{10,11... | collective-permute-start | bytes 1572872 | tf_op jit(solution)/shard_map/ppermute | solution.py:18
  14.0 0.8 copy-start.11
  39.5 2.9 %copy-start = (f32[128,16,128]{0,2,1:T(8,128)S(1)}, f32[128,16,128]{0,2,1:T(8,128)}, u32[]{:S(2)}) copy-start(f32[128,16,128]{0,2,1:T(8,128)} %broadcast_multiply_fusion.2) | copy-start | bytes 3145732
  39.5 2.9 %copy-start.3 = (f32[1,1,128,2048]{2,3,1,0:T(8,128)S(1)}, f32[1,1,128,2048]{2,3,1,0:T(8,128)}, u32[]{:S(2)}) copy-start(f32[1,1,128,2048]{2,3,1,0:T(8,128)} %copy.53) | copy-start | bytes 3145732
  39.5 3.2 %copy-start.5 = (f32[16,128,256]{2,1,0:T(8,128)S(1)}, f32[16,128,256]{2,1,0:T(8,128)}, u32[]{:S(2)}) copy-start(f32[16,128,256]{2,1,0:T(8,128)} %get-tuple-element.24) | copy-start | bytes 6291460
  47.6 1.9 copy-start.2
  50.5 30.6 %collective-permute-start.2 = (bf16[128,16,128]{0,2,1:T(8,128)(2,1)}, bf16[128,16,128]{0,2,1:T(8,128)(2,1)}, u32[]{:S(2)}, u32[]{:S(2)}) collective-permute-start(bf16[128,16,128]{0,2,1:T(8,128)(2,1)} %multiply_convert_fusion.7), channel_id=1, source_target_pairs={{0,1},{1,0},{2,3},{3,2},{4,5},{5,4},{6,7},{7,6},{8,9},{9,8},{10,11... | collective-permute-start | bytes 1572872 | tf_op jit(solution)/shard_map/ppermute | solution.py:18
  87.3 34.4 %collective-permute-start.3 = (f32[128,2048]{1,0:T(8,128)}, f32[128,2048]{1,0:T(8,128)}, u32[]{:S(2)}, u32[]{:S(2)}) collective-permute-start(f32[128,2048]{1,0:T(8,128)} %copy.62), channel_id=1, source_target_pairs={{16,0},{32,16},{48,32},{64,48},{80,64},{96,80},{112,96},{128,112},... | collective-permute-start | bytes 3145736 | tf_op jit(solution)/shard_map/ppermute | solution.py:24
  100.1 4.8 %copy-start.1 = (f32[128,16,128]{0,2,1:T(8,128)S(1)}, f32[128,16,128]{0,2,1:T(8,128)}, u32[]{:S(2)}) copy-start(f32[128,16,128]{0,2,1:T(8,128)} %broadcast_multiply_fusion.2) | copy-start | bytes 3145732
  100.1 4.8 %copy-start.4 = (f32[1,1,128,2048]{2,3,1,0:T(8,128)S(1)}, f32[1,1,128,2048]{2,3,1,0:T(8,128)}, u32[]{:S(2)}) copy-start(f32[1,1,128,2048]{2,3,1,0:T(8,128)} %copy.53) | copy-start | bytes 3145732
  104.9 16.8 %copy-start.10 = (bf16[1,1,128,2048]{3,2,1,0:T(8,128)(2,1)S(1)}, bf16[1,1,128,2048]{3,2,1,0:T(8,128)(2,1)}, u32[]{:S(2)}) copy-start(bf16[1,1,128,2048]{3,2,1,0:T(8,128)(2,1)} %param.8) | copy-start | bytes 1572868
  107.5 16.9 %copy-start.6 = (f32[16,128,256]{2,1,0:T(8,128)S(1)}, f32[16,128,256]{2,1,0:T(8,128)}, u32[]{:S(2)}) copy-start(f32[16,128,256]{2,1,0:T(8,128)} %get-tuple-element.29) | copy-start | bytes 6291460
  127.8 1.2 copy-start.7
  127.8 1.5 copy-start.8
  130.0 1.2 copy-start.9
where the time goes:
time: 221 us; the launch traced here: 220 us
  blocking collectives  86.5 us (39%)
  waiting for transfers between devices  49.7 us (22%)
  starting transfers between devices  27.7 us (13%)
  matrix products  27.2 us (12%)
  other arithmetic  14.5 us (7%)
  local copies, waits for them, and re-layouts  14.3 us (6%)
    psum x1, blocking collectives, shards(): summed = lax.psum(totals.reshape(4, channels), ('dp', 'seq'))  86.5 us
    ppermute x3, waiting for transfers between devices, partner(): return lax.ppermute(block, axis, route)  35.5 us
    ppermute x3, starting transfers between devices, partner(): return lax.ppermute(block, axis, route)  16 us
    ppermute x1, waiting for transfers between devices, from_behind(): return lax.ppermute(block, axis, route)  14.2 us
    ppermute x1, starting transfers between devices, from_behind(): return lax.ppermute(block, axis, route)  11.7 us
    sub x2, matrix products, attend(): exped = jnp.exp(scores - jnp.max(scores, axis=-1, keepdims=True))  8.66 us
    dot_general x2, matrix products, attend(): jnp.einsum('thd,shd->hts', grad_out, val_mat, preferred_element_type=jnp....  5.55 us
  transfers between devices with their start and end apart: 4, of which 3 were waited for; matrix products, arithmetic and copies ran while one was open for 16% of the time, Pallas kernels for 0%

commit v1 on v0

--- a/solution.py
+++ b/solution.py
@@ -149,7 +149,9 @@
                 uppermost_result_derivative[step_index, 0].astype(jnp.float32),
                 received,
             )
-    summed = lax.psum(totals.reshape(4, channels), ("dp", "seq"))
+    x = totals.reshape(4, channels)
+    parts = lax.all_gather(x, ("dp", "seq"), axis=0, tiled=False)
+    summed = parts.sum(axis=0)
     return summed[None]
 
 

time: 221 us -> 188 us (0.85)
  the two profiles are of different devices: /device:TPU:24 before, /device:TPU:56 now
where the time goes in v1:
time: 188 us; the launch traced here: 187 us
  blocking collectives  54.4 us (29%)
  waiting for transfers between devices  51 us (27%)
  matrix products  27.2 us (14%)
  starting transfers between devices  24.9 us (13%)
  other arithmetic  15.2 us (8%)
  local copies, waits for them, and re-layouts  14.3 us (8%)
    all_gather x1, blocking collectives, shards(): parts = lax.all_gather(x, ('dp', 'seq'), axis=0, tiled=False)  54.4 us
    ppermute x3, waiting for transfers between devices, partner(): return lax.ppermute(block, axis, route)  37.9 us
    ppermute x3, starting transfers between devices, partner(): return lax.ppermute(block, axis, route)  13.2 us
    ppermute x1, waiting for transfers between devices, from_behind(): return lax.ppermute(block, axis, route)  13.1 us
    ppermute x1, starting transfers between devices, from_behind(): return lax.ppermute(block, axis, route)  11.7 us
    sub x2, matrix products, attend(): exped = jnp.exp(scores - jnp.max(scores, axis=-1, keepdims=True))  8.66 us
    dot_general x2, matrix products, attend(): jnp.einsum('thd,shd->hts', grad_out, val_mat, preferred_element_type=jnp....  5.55 us
    dot_general x2, matrix products, shards(): jnp.einsum('hts,thd->shd', probs_low, grad_out, preferred_element_type=jn...  4 us
  transfers between devices with their start and end apart: 4, of which 3 were waited for; matrix products, arithmetic and copies ran while one was open for 18% of the time, Pallas kernels for 0%

profile of v1, /device:TPU:56, one launch (start us, length us, event | category | flops | bytes accessed | tf_op | source)
XLA Modules:
  0.0 187.2 jit_solution(14784241271362220789)
XLA Ops:
  0.0 2.7 %slice_convert_fusion = (f32[1,1,1,128,2048]{4,3,2,1,0:T(8,128)}, bf16[128,2048]{1,0:T(8,128)(2,1)}, bf16[128,2048]{1,0:T(8,128)(2,1)}, f32[1,1,1,128,2048]{4,3,2,1,0:T(8,128)S(1)}) fusion(bf16[1,2,1,128,2048]{4,3,2,1,0:T(8,128)(2,1)} %param.6), kind=kLoop, calls=%fused_computation.75 | loop fusion | flops 524288 | bytes 4194304 | tf_op jit(solution)/shard_map/convert_element_type | solution.py:28
  2.7 4.7 %collective-permute-start = (bf16[128,2048]{1,0:T(8,128)(2,1)}, bf16[128,2048]{1,0:T(8,128)(2,1)}, u32[]{:S(2)}, u32[]{:S(2)}) collective-permute-start(bf16[128,2048]{1,0:T(8,128)(2,1)} %get-tuple-element.12), channel_id=1, source_target_pairs={{0,1},{1,0},{2,3},{3,2},{4,5},{5,4},{6,7},{7,6},{8,9},{9,8},{10,11... | collective-permute-start | bytes 1572872 | tf_op jit(solution)/shard_map/ppermute | solution.py:18
  7.4 5.0 %collective-permute-start.1 = (bf16[128,2048]{1,0:T(8,128)(2,1)}, bf16[128,2048]{1,0:T(8,128)(2,1)}, u32[]{:S(2)}, u32[]{:S(2)}) collective-permute-start(bf16[128,2048]{1,0:T(8,128)(2,1)} %get-tuple-element.13), channel_id=1, source_target_pairs={{0,1},{1,0},{2,3},{3,2},{4,5},{5,4},{6,7},{7,6},{8,9},{9,8},{10,11... | collective-permute-start | bytes 1572872 | tf_op jit(solution)/shard_map/ppermute | solution.py:18
  14.8 1.5 copy.79
  16.6 2.3 %copy.74 = f32[1,1,128,2048]{2,3,1,0:T(8,128)} copy(bf16[1,1,128,2048]{3,2,1,0:T(8,128)(2,1)} %param.7) | data formatting | bytes 1572864 | tf_op jit(solution)/shard_map/convert_element_type | solution.py:97
  20.6 13.8 %collective-permute-done = bf16[128,2048]{1,0:T(8,128)(2,1)} collective-permute-done((bf16[128,2048]{1,0:T(8,128)(2,1)}, bf16[128,2048]{1,0:T(8,128)(2,1)}, u32[]{:S(2)}, u32[]{:S(2)}) %collective-permute-start) | collective-permute-done | bytes 524320 | tf_op jit(solution)/shard_map/ppermute | solution.py:18
  36.9 3.9 %fusion.48 = (f32[16,128]{1,0:T(8,128)S(1)}, f32[16,128,256]{2,1,0:T(8,128)}) fusion(pred[256]{0:T(512)(128)(4,1)S(1)} %broadcast_bitcast_fusion.1, f32[16,128]{1,0:T(8,128)S(1)} %bitcast.123, f32[128,16,128]{0,2,1:T(8,128)} %broadcast_multiply_fusion.2, f32[128,16,128]{0,2,1:T(8,128)S(1)} %broadcast_multiply_fusion.3, f32[16,128]{1,0:T(8,128)S(1)} %bitcast.118), kind=kOutput, calls=%fused_computation.118 | convolution fusion | flops 138412288 | bytes 4219136 | tf_op jit(solution)/shard_map/sub | solution.py:66
  40.8 2.8 %fusion.26 = f32[16,128,256]{2,1,0:T(8,128)S(1)} fusion(f32[128,16,128]{0,2,1:T(8,128)} %bitcast.109, f32[16,128]{1,0:T(8,128)S(1)} %bitcast.140, f32[16,128,256]{2,1,0:T(8,128)} %get-tuple-element.24, f32[16,128]{1,0:T(8,128)S(1)} %get-tuple-element.23), kind=kOutput, calls=%fused_computation.70 | convolution fusion | flops 135790592 | bytes 5259264 | tf_op jit(solution)/shard_map/hts,thd->shd/dot_general | solution.py:121
  43.9 2.2 %multiply_reduce_fusion.1 = (f32[16,128]{1,0:T(8,128)S(1)}, f32[16,128,256]{2,1,0:T(8,128)S(1)}) fusion(f32[16,128,256]{2,1,0:T(8,128)S(1)} %copy-done.5, f32[16,128]{1,0:T(8,128)S(1)} %get-tuple-element.23, f32[16,128]{1,0:T(8,128)S(1)} %bitcast.130, f32[128,16,128]{0,2,1:T(8,128)S(1)} %copy-done, f32[128,16,128]{0,2,1:T(8,128)S(1)} %broadcast_multiply_fusion.3, ...), kind=kOutput, calls=%fused_computation.23 | convolution fusion | flops 137885696 | bytes 7372800 | tf_op jit(solution)/shard_map/thd,shd->hts/dot_general | solution.py:71
  46.9 1.9 %fusion.5 = (f32[16,128]{1,0:T(8,128)S(1)}, f32[16,128]{1,0:T(8,128)S(1)}, f32[256,16,128]{0,2,1:T(8,128)S(1)}) fusion(f32[128,16,128]{0,2,1:T(8,128)S(1)} %copy-done, f32[128,16,128]{0,2,1:T(8,128)S(1)} %broadcast_multiply_fusion.3, f32[16,128,256]{2,1,0:T(8,128)S(1)} %fusion.26, f32[16,128]{1,0:T(8,128)S(1)} %bitcast.131, ...), kind=kOutput, calls=%fused_computation.15 | convolution fusion | flops 139456512 | bytes 7380992 | tf_op jit(solution)/shard_map/hts,thd->shd/dot_general | solution.py:118
  48.8 1.9 %multiply_reduce_fusion.3 = (f32[128,16]{0,1:T(8,128)S(1)}, f32[128,16]{0,1:T(8,128)S(1)}, f32[16,128]{1,0:T(8,128)S(1)}, f32[16,128,128]{2,1,0:T(8,128)}) fusion(f32[128,16,128]{0,2,1:T(8,128)S(1)} %broadcast_multiply_fusion.3, f32[256,16,128]{0,2,1:T(8,128)S(1)} %get-tuple-element.10, f32[16,128]{1,0:T(8,128)S(1)} %broadcast_multiply_fusion.5, ...), kind=kOutput, calls=%fused_computation.48 | convolution fusion | flops 138143744 | bytes 8429568 | tf_op jit(solution)/shard_map/hts,shd->thd/dot_general | solution.py:114
  51.8 3.5 %collective-permute-start.2 = (bf16[128,16,128]{0,2,1:T(8,128)(2,1)}, bf16[128,16,128]{0,2,1:T(8,128)(2,1)}, u32[]{:S(2)}, u32[]{:S(2)}) collective-permute-start(bf16[128,16,128]{0,2,1:T(8,128)(2,1)} %multiply_convert_fusion.7), channel_id=1, source_target_pairs={{0,1},{1,0},{2,3},{3,2},{4,5},{5,4},{6,7},{7,6},{8,9},{9,8},{10,11... | collective-permute-start | bytes 1572872 | tf_op jit(solution)/shard_map/ppermute | solution.py:18
  55.3 1.2 copy.80
  56.7 24.1 %collective-permute-done.2 = bf16[128,16,128]{0,2,1:T(8,128)(2,1)} collective-permute-done((bf16[128,16,128]{0,2,1:T(8,128)(2,1)}, bf16[128,16,128]{0,2,1:T(8,128)(2,1)}, u32[]{:S(2)}, u32[]{:S(2)}) %collective-permute-start.2) | collective-permute-done | bytes 524320 | tf_op jit(solution)/shard_map/ppermute | solution.py:18
  80.7 3.6 %convert_add_fusion = f32[128,16,128]{0,2,1:T(8,128)} fusion(bf16[128,16,128]{0,2,1:T(8,128)(2,1)} %collective-permute-done.2, f32[128,16,128]{0,2,1:T(8,128)} %bitcast.110, f32[128,16]{0,1:T(8,128)S(1)} %broadcast_multiply_fusion.7, f32[128,16]{0,1:T(8,128)S(1)} %add_rsqrt_fusion.3, f32[256,16,128]{0,2,1:T(8,128)} %copy-done.2, ...), kind=kLoop, calls=%fused_computation.45 | loop fusion | flops 2359296 | bytes 5791744 | tf_op jit(solution)/shard_map/add | solution.py:142
  84.3 2.6 %copy.83 = f32[128,2048]{1,0:T(8,128)} copy(f32[128,2048]{0,1:T(8,128)} %bitcast.113) | data formatting | bytes 2097152 | tf_op jit(solution)/shard_map/reshape | solution.py:146
  86.9 11.7 %collective-permute-start.3 = (f32[128,2048]{1,0:T(8,128)}, f32[128,2048]{1,0:T(8,128)}, u32[]{:S(2)}, u32[]{:S(2)}) collective-permute-start(f32[128,2048]{1,0:T(8,128)} %copy.83), channel_id=1, source_target_pairs={{16,0},{32,16},{48,32},{64,48},{80,64},{96,80},{112,96},{128,112},... | collective-permute-start | bytes 3145736 | tf_op jit(solution)/shard_map/ppermute | solution.py:24
  99.7 4.8 %fusion.49 = (f32[16,128]{1,0:T(8,128)S(1)}, f32[16,128,256]{2,1,0:T(8,128)}) fusion(pred[256]{0:T(512)(128)(4,1)S(1)} %broadcast_bitcast_fusion, f32[16,128]{1,0:T(8,128)S(1)} %bitcast.125, f32[128,16,128]{0,2,1:T(8,128)} %broadcast_multiply_fusion, f32[128,16,128]{0,2,1:T(8,128)} %broadcast_multiply_fusion.1, f32[16,128]{1,0:T(8,128)S(1)} %bitcast.120), kind=kOutput, calls=%fused_computation.119 | convolution fusion | flops 138412288 | bytes 4219136 | tf_op jit(solution)/shard_map/sub | solution.py:66
  104.5 2.6 %fusion.12 = f32[16,128]{1,0:T(8,128)S(1)} fusion(f32[128,16,128]{0,2,1:T(8,128)S(1)} %bitcast.112, f32[16,128]{1,0:T(8,128)S(1)} %bitcast.132, f32[128,16,128]{0,2,1:T(8,128)S(1)} %copy-done.1, f32[128,16,128]{0,2,1:T(8,128)S(1)} %broadcast_multiply_fusion.3, f32[16,128,256]{2,1,0:T(8,128)} %get-tuple-element.24, f32[16,128]{1,0:T(8,128)S(1)} %get-tuple-element.23), kind=kOutput, calls=%fused_computation.37 | convolution fusion | flops 137361408 | bytes 5267456 | tf_op jit(solution)/shard_map/hts,shd->thd/dot_general | solution.py:69
  107.1 13.1 %collective-permute-done.3 = f32[128,2048]{1,0:T(8,128)} collective-permute-done((f32[128,2048]{1,0:T(8,128)}, f32[128,2048]{1,0:T(8,128)}, u32[]{:S(2)}, u32[]{:S(2)}) %collective-permute-start.3) | collective-permute-done | bytes 1048608 | tf_op jit(solution)/shard_map/ppermute | solution.py:24
  120.2 1.3 convert_select_fusion
  121.5 1.3 copy.84
  122.9 3.4 %multiply_reduce_fusion = (f32[16,128]{1,0:T(8,128)S(1)}, f32[16,128,256]{2,1,0:T(8,128)S(1)}) fusion(f32[16,128,256]{2,1,0:T(8,128)S(1)} %copy-done.6, f32[16,128]{1,0:T(8,128)S(1)} %get-tuple-element.28, f32[16,128]{1,0:T(8,128)S(1)} %bitcast.133, f32[128,16,128]{0,2,1:T(8,128)} %broadcast_multiply_fusion, f32[128,16,128]{0,2,1:T(8,128)} %broadcast_multiply_fusion.1, ...), kind=kOutput, calls=%fused_computation.17 | convolution fusion | flops 137885696 | bytes 7372800 | tf_op jit(solution)/shard_map/thd,shd->hts/dot_general | solution.py:71
  132.1 54.4 %all_gather.3 = f32[16,4,2048]{2,1,0:T(4,128)S(1)} all-gather(f32[1,4,2048]{2,1,0:T(4,128)S(1)} %maximum_add_fusion), channel_id=1, replica_groups=mesh['segment'=32,'dp'=8,'seq'=2] {'dp','seq'}, dimensions={0}, use_global_device_ids=true | all-gather | bytes 557056 | tf_op jit(solution)/shard_map/all_gather | solution.py:153
  (69 shorter events, 16.4 us)
Async XLA Ops:
  0.0 12.8 %copy-start.13 = (s32[1,2,1,2]{3,2,1,0:T(1,128)S(1)}, s32[1,2,1,2]{3,2,1,0:T(1,128)}, u32[]{:S(2)}) copy-start(s32[1,2,1,2]{3,2,1,0:T(1,128)} %param.11) | copy-start | bytes 52
  0.0 12.8 %copy-start.12 = (s32[1,2,1,2,2]{4,3,2,1,0:T(2,128)S(1)}, s32[1,2,1,2,2]{4,3,2,1,0:T(2,128)}, u32[]{:S(2)}) copy-start(s32[1,2,1,2,2]{4,3,2,1,0:T(2,128)} %param.10) | copy-start | bytes 100
  2.7 31.7 %collective-permute-start = (bf16[128,2048]{1,0:T(8,128)(2,1)}, bf16[128,2048]{1,0:T(8,128)(2,1)}, u32[]{:S(2)}, u32[]{:S(2)}) collective-permute-start(bf16[128,2048]{1,0:T(8,128)(2,1)} %get-tuple-element.12), channel_id=1, source_target_pairs={{0,1},{1,0},{2,3},{3,2},{4,5},{5,4},{6,7},{7,6},{8,9},{9,8},{10,11... | collective-permute-start | bytes 1572872 | tf_op jit(solution)/shard_map/ppermute | solution.py:18
  7.4 47.9 %collective-permute-start.1 = (bf16[128,2048]{1,0:T(8,128)(2,1)}, bf16[128,2048]{1,0:T(8,128)(2,1)}, u32[]{:S(2)}, u32[]{:S(2)}) collective-permute-start(bf16[128,2048]{1,0:T(8,128)(2,1)} %get-tuple-element.13), channel_id=1, source_target_pairs={{0,1},{1,0},{2,3},{3,2},{4,5},{5,4},{6,7},{7,6},{8,9},{9,8},{10,11... | collective-permute-start | bytes 1572872 | tf_op jit(solution)/shard_map/ppermute | solution.py:18
  14.0 0.8 copy-start.11
  40.8 2.9 %copy-start = (f32[128,16,128]{0,2,1:T(8,128)S(1)}, f32[128,16,128]{0,2,1:T(8,128)}, u32[]{:S(2)}) copy-start(f32[128,16,128]{0,2,1:T(8,128)} %broadcast_multiply_fusion.2) | copy-start | bytes 3145732
  40.8 2.9 %copy-start.3 = (f32[1,1,128,2048]{2,3,1,0:T(8,128)S(1)}, f32[1,1,128,2048]{2,3,1,0:T(8,128)}, u32[]{:S(2)}) copy-start(f32[1,1,128,2048]{2,3,1,0:T(8,128)} %copy.74) | copy-start | bytes 3145732
  40.8 3.2 %copy-start.5 = (f32[16,128,256]{2,1,0:T(8,128)S(1)}, f32[16,128,256]{2,1,0:T(8,128)}, u32[]{:S(2)}) copy-start(f32[16,128,256]{2,1,0:T(8,128)} %get-tuple-element.24) | copy-start | bytes 6291460
  48.8 1.9 %copy-start.2 = (f32[256,16,128]{0,2,1:T(8,128)}, f32[256,16,128]{0,2,1:T(8,128)S(1)}, u32[]{:S(2)}) copy-start(f32[256,16,128]{0,2,1:T(8,128)S(1)} %get-tuple-element.10) | copy-start | bytes 6291460
  51.8 29.0 %collective-permute-start.2 = (bf16[128,16,128]{0,2,1:T(8,128)(2,1)}, bf16[128,16,128]{0,2,1:T(8,128)(2,1)}, u32[]{:S(2)}, u32[]{:S(2)}) collective-permute-start(bf16[128,16,128]{0,2,1:T(8,128)(2,1)} %multiply_convert_fusion.7), channel_id=1, source_target_pairs={{0,1},{1,0},{2,3},{3,2},{4,5},{5,4},{6,7},{7,6},{8,9},{9,8},{10,11... | collective-permute-start | bytes 1572872 | tf_op jit(solution)/shard_map/ppermute | solution.py:18
  86.9 33.2 %collective-permute-start.3 = (f32[128,2048]{1,0:T(8,128)}, f32[128,2048]{1,0:T(8,128)}, u32[]{:S(2)}, u32[]{:S(2)}) collective-permute-start(f32[128,2048]{1,0:T(8,128)} %copy.83), channel_id=1, source_target_pairs={{16,0},{32,16},{48,32},{64,48},{80,64},{96,80},{112,96},{128,112},... | collective-permute-start | bytes 3145736 | tf_op jit(solution)/shard_map/ppermute | solution.py:24
  99.7 4.8 %copy-start.1 = (f32[128,16,128]{0,2,1:T(8,128)S(1)}, f32[128,16,128]{0,2,1:T(8,128)}, u32[]{:S(2)}) copy-start(f32[128,16,128]{0,2,1:T(8,128)} %broadcast_multiply_fusion.2) | copy-start | bytes 3145732
  99.7 4.8 %copy-start.4 = (f32[1,1,128,2048]{2,3,1,0:T(8,128)S(1)}, f32[1,1,128,2048]{2,3,1,0:T(8,128)}, u32[]{:S(2)}) copy-start(f32[1,1,128,2048]{2,3,1,0:T(8,128)} %copy.74) | copy-start | bytes 3145732
  104.5 15.7 %copy-start.10 = (bf16[1,1,128,2048]{3,2,1,0:T(8,128)(2,1)S(1)}, bf16[1,1,128,2048]{3,2,1,0:T(8,128)(2,1)}, u32[]{:S(2)}) copy-start(bf16[1,1,128,2048]{3,2,1,0:T(8,128)(2,1)} %param.8) | copy-start | bytes 1572868
  107.1 15.8 %copy-start.6 = (f32[16,128,256]{2,1,0:T(8,128)S(1)}, f32[16,128,256]{2,1,0:T(8,128)}, u32[]{:S(2)}) copy-start(f32[16,128,256]{2,1,0:T(8,128)} %get-tuple-element.29) | copy-start | bytes 6291460
  126.2 1.2 copy-start.7
  126.2 1.5 copy-start.8
  128.5 1.2 copy-start.9
